TPU v7x, 256 devices: a whole 4x4x8 slice. The times are simulated.
256 devices in a mesh: batch: 8 (over z), col: 32 (over y, x, core).
Axes of the slice: x: 4, y: 4, z: 8, core: 2. Of those that a mesh axis runs over, the one named last changes fastest.
Arguments:
- views: bfloat16 [2, 1024, 4096], P(None, 'batch', 'col'), may hold values from -132 to 132
- norm_scale_gain: float32 [4096], P('col'), may hold values from 0.5 to 1.5
- norm_shift_bias: float32 [4096], P('col'), may hold values from -3 to 3
- weight: bfloat16 [4096, 8192], P(None, 'col'), may hold values from -0.09375 to 0.09375
Outputs:
- loss: float32 [], replicated
- grad_weight: float32 [4096, 8192], P('batch', 'col')
- grad_gain: float32 [4096], P('col')
- grad_bias: float32 [4096], P('col')
- views_gradient: float32 [2, 1024, 4096], P(None, 'batch', 'col')
All inputs are finite; a program needn't handle non-finite values.
Results may differ from a plain program's by a relative error of at most 0.0027.
Values may be sent and summed in bfloat16 or wider, within the bound.
A program may use at most 64 MiB of HBM per device.

v0:
```python
import jax
import jax.numpy as jnp
from jax import lax
from jax.sharding import PartitionSpec as P

E = 8192
eps_norm = 1e-05
eps_std = 0.0001


def gelu_slope(preactivation):
    value, pullback = jax.vjp(lambda t: jax.nn.gelu(t, approximate=True), preactivation)
    return pullback(jnp.ones_like(value))[0]


def shards(views, norm_scale_gain, norm_shift_bias, weight):
    n_batch = lax.axis_size("batch")
    n_col = lax.axis_size("col")
    local_rows = views.shape[1]
    sample_count = local_rows * n_batch
    scale = sample_count * E / 128.0
    hidden_float = views.astype(jnp.float32)
    total = lax.psum(jnp.sum(hidden_float, axis=1), "batch")
    batch_average = total[:, None, :] / sample_count
    centred = hidden_float - batch_average
    spread = lax.psum(jnp.sum(centred * centred, axis=1), "batch")
    var = spread[:, None, :] / sample_count
    inverse_deviation = 1.0 / jnp.sqrt(var + eps_norm)
    normalised_input = (hidden_float - batch_average) * inverse_deviation
    preactivation = norm_scale_gain * normalised_input + norm_shift_bias
    act = jax.nn.gelu(preactivation, approximate=True).astype(jnp.bfloat16)
    act_full = lax.all_gather(act, "col", axis=2, tiled=True)
    z_local = jnp.einsum(
        "vrk,kj->vrj", act_full, weight, preferred_element_type=jnp.float32
    ).astype(jnp.bfloat16)
    z_all = lax.all_gather(z_local, "batch", axis=1, tiled=True)
    zf_all = z_all.astype(jnp.float32)
    zmean = jnp.mean(zf_all, axis=1, keepdims=True)
    zc_all = zf_all - zmean
    zvar = jnp.sum(zc_all * zc_all, axis=1, keepdims=True) / (sample_count - 1)
    std = jnp.sqrt(zvar + eps_std)
    zcb_all = zc_all.astype(jnp.bfloat16)
    offset = lax.axis_index("batch") * local_rows
    zc_loc = lax.dynamic_slice_in_dim(zc_all, offset, local_rows, 1)
    zcb_loc = zc_loc.astype(jnp.bfloat16)
    diag = jnp.sum(jnp.square(zcb_all.astype(jnp.float32)), axis=1, keepdims=True)
    kernel_part = jnp.einsum("vrj,vmj->vrm", zcb_loc, zcb_all, preferred_element_type=jnp.float32)
    kernel = lax.psum(kernel_part, "col")
    kernel_b = kernel.astype(jnp.bfloat16)
    denom = float((sample_count - 1) ** 2 * E)
    coef = 4.0 * scale / denom
    hinge_coef = 25.0 * scale / (2.0 * E * (sample_count - 1))
    mask = jnp.where(std < 1.0, 1.0, 0.0)
    moved = jnp.einsum("vrm,vmj->vrj", kernel_b, zcb_all, preferred_element_type=jnp.float32)
    g_cov = coef * (moved - zcb_loc.astype(jnp.float32) * diag)
    g_var = -hinge_coef * mask * zc_loc / std
    summed = g_cov + g_var
    col_total = lax.psum(jnp.sum(summed, axis=1), "batch")
    zf_loc = z_local.astype(jnp.float32)
    diff = zf_loc[0] - zf_loc[1]
    g_inv = 50.0 * scale / (sample_count * E) * diff
    dz = summed - col_total[:, None, :] / sample_count + jnp.stack([g_inv, -g_inv])
    dzb = dz.astype(jnp.bfloat16)
    inv_share = jnp.sum(diff * diff) / (sample_count * E)
    hinge_share = jnp.sum(jnp.maximum(1.0 - std, 0.0)) / (2 * E)
    block_share = jnp.sum(kernel * kernel) / denom
    diag_share = jnp.sum(diag * diag) / denom
    share = 25.0 * inv_share + (25.0 * hinge_share - diag_share) / n_batch + block_share / n_col
    loss = lax.psum(share, ("batch", "col"))
    d_act_t = lax.psum_scatter(
        jnp.einsum("kj,vrj->kvr", weight, dzb, preferred_element_type=jnp.float32),
        "col",
        scatter_dimension=0,
        tiled=True,
    )
    d_act = jnp.transpose(d_act_t, (1, 2, 0))
    grad_weight = lax.psum_scatter(
        jnp.einsum("vrk,vrj->kj", act_full, dzb, preferred_element_type=jnp.float32),
        "batch",
        scatter_dimension=0,
        tiled=True,
    )
    preactivation_gradient = d_act * gelu_slope(preactivation)
    bias_gradient_sum, gain_gradient_sum = lax.psum(
        (
            jnp.sum(preactivation_gradient, axis=1),
            jnp.sum(preactivation_gradient * normalised_input, axis=1),
        ),
        "batch",
    )
    grad_bias = jnp.sum(bias_gradient_sum, axis=0)
    grad_gain = jnp.sum(gain_gradient_sum, axis=0)
    views_gradient = (
        norm_scale_gain
        * (
            preactivation_gradient
            - bias_gradient_sum[:, None, :] / sample_count
            - normalised_input * gain_gradient_sum[:, None, :] / sample_count
        )
        * inverse_deviation
    )
    return (loss, grad_weight, grad_gain, grad_bias, views_gradient)


def solution(mesh):
    placed = (P(None, "batch", "col"), P("col"), P("col"), P(None, "col"))
    return jax.shard_map(
        shards,
        mesh=mesh,
        in_specs=placed,
        out_specs=(P(), P("batch", "col"), P("col"), P("col"), P(None, "batch", "col")),
        check_vma=False,
    )
```

profile of v0, /device:TPU:1, one launch (start us, length us, event | category | flops | bytes accessed | tf_op | source)
XLA Modules:
  0.0 430.3 jit_solution(8545685748164966906)
XLA Ops:
  7.2 0.0 copy-start
  7.2 0.0 all-gather.3.cloned.1.call-start
  7.2 1.0 convert_reduce_fusion.1
  8.2 17.3 %psum.49 = f32[2,128]{1,0:T(2,128)S(1)} all-reduce(f32[2,128]{1,0:T(2,128)S(1)} %convert_reduce_fusion.1), channel_id=1, replica_groups=mesh['batch'=8,'col'=32] {'batch'}, use_global_device_ids=true, to_apply=%region_1.0 | all-reduce | flops 256 | bytes 2048 | tf_op jit(solution)/shard_map/psum | solution.py:23
  25.5 0.9 fusion.32
  26.4 10.8 %psum.50 = f32[2,128]{1,0:T(2,128)S(1)} all-reduce(f32[2,128]{1,0:T(2,128)S(1)} %fusion.32), channel_id=1, replica_groups=mesh['batch'=8,'col'=32] {'batch'}, use_global_device_ids=true, to_apply=%region_3.0 | all-reduce | flops 256 | bytes 2048 | tf_op jit(solution)/shard_map/psum | solution.py:26
  37.2 1.6 fusion.25
  38.8 0.0 all-gather.3.cloned.1.call-update
  38.8 0.0 all-gather.5.cloned.1.call-start
  38.8 56.4 %all-gather.3.cloned.1.call-done = bf16[2,128,4096]{2,1,0:T(8,128)(2,1)} async-done(((bf16[2,128,128]{2,1,0:T(8,128)(2,1)}), bf16[2,128,4096]{2,1,0:T(8,128)(2,1)}) %all-gather.3.cloned.1.call-update) | async-done | bytes 2097168 | tf_op jit(solution)/shard_map/all_gather | solution.py:32
  95.2 0.0 copy-done
  95.2 3.0 fusion.42
  98.2 0.0 all-gather.5.cloned.1.call-update
  98.2 0.0 all-reduce.3.cloned.1.call-start
  98.2 32.8 %all-gather.5.cloned.1.call-done = bf16[2,1024,256]{2,1,0:T(8,128)(2,1)} async-done(((bf16[2,128,256]{2,1,0:T(8,128)(2,1)}), bf16[2,1024,256]{2,1,0:T(8,128)(2,1)}) %all-gather.5.cloned.1.call-update) | async-done | bytes 1048592 | tf_op jit(solution)/shard_map/all_gather | solution.py:36
  131.1 0.0 copy-start.1
  131.1 1.5 convert_reduce_fusion
  132.6 2.1 multiply_reduce_fusion
  134.6 0.0 copy-start.2
  134.7 1.3 copy-done.2
  136.0 0.0 copy-done.1
  136.0 1.5 fusion.10
  137.5 0.0 all-reduce.3.cloned.1.call-update
  137.5 0.0 reduce-scatter.5.cloned.1.call-start
  137.6 1.3 fusion.41
  138.8 0.0 copy-start.5
  138.8 1.3 fusion.37
  140.2 115.7 %all-reduce.3.cloned.1.call-done = f32[2,128,1024]{2,1,0:T(8,128)} async-done(((f32[2,128,1024]{2,1,0:T(8,128)}), f32[2,128,1024]{2,1,0:T(8,128)}) %all-reduce.3.cloned.1.call-update) | async-done | bytes 1048592 | tf_op jit(solution)/shard_map/psum | solution.py:48
  255.9 2.4 fusion.43
  258.3 13.7 %psum.53 = f32[2,256]{1,0:T(2,128)S(1)} all-reduce(f32[2,256]{1,0:T(2,128)S(1)} %get-tuple-element.23), channel_id=1, replica_groups=mesh['batch'=8,'col'=32] {'batch'}, use_global_device_ids=true, to_apply=%region_14.15 | all-reduce | flops 512 | bytes 4096 | tf_op jit(solution)/shard_map/psum | solution.py:58
  272.0 0.0 copy-done.5
  272.0 1.0 fusion.13
  272.9 2.7 convolution_bitcast_fusion
  275.7 0.0 reduce-scatter.5.cloned.1.call-update
  275.7 0.0 reduce-scatter.3.cloned.1.call-start
  275.7 4.3 convolution_bitcast_fusion.1
  280.0 0.0 copy-start.4
  280.0 0.0 copy-start.3
  280.0 0.0 copy-start.6
  280.0 0.0 copy-start.7
  280.0 0.0 reduce-scatter.3.cloned.1.call-update
  281.4 0.6 multiply_reduce_fusion.4
  282.7 0.0 copy-done.4
  282.7 0.9 multiply_reduce_fusion.2
  284.2 78.4 %psum.52 = f32[]{:T(128)} all-reduce(f32[]{:T(128)S(6)} %add.83), channel_id=1, replica_groups=mesh['batch'=8,'col'=32] {'batch','col'}, use_global_device_ids=true, to_apply=%region_12.13 | all-reduce | flops 1 | bytes 8 | tf_op jit(solution)/shard_map/psum | solution.py:69
  362.6 1.7 reduce-scatter.5.cloned.1.call-done
  364.4 0.0 copy-done.3
  364.4 0.0 copy-done.6
  364.4 0.0 copy-done.7
  364.4 1.0 fusion.39
  365.4 14.1 %all-reduce = (f32[2,128]{1,0:T(2,128)S(1)}, f32[2,128]{1,0:T(2,128)S(1)}) all-reduce(f32[2,128]{1,0:T(2,128)S(1)} %get-tuple-element.8, f32[2,128]{1,0:T(2,128)S(1)} %get-tuple-element.7), channel_id=1, replica_groups=mesh['batch'=8,'col'=32] {'batch'}, use_global_device_ids=true, to_apply=%region_18.19 | all-reduce | flops 512 | bytes 4096 | tf_op jit(solution)/shard_map/psum | solution.py:84
  379.5 0.5 reduce_sum.137
  380.1 0.5 broadcast_multiply_fusion.3
  380.6 0.7 fusion.31
  381.3 42.5 %reduce-scatter.3.cloned.1.call-done = f32[512,256]{1,0:T(8,128)} async-done(((f32[4096,256]{1,0:T(8,128)}), f32[512,256]{1,0:T(8,128)}) %reduce-scatter.3.cloned.1.call-update) | async-done | bytes 524304 | tf_op jit(solution)/shard_map/reduce_scatter | solution.py:77
  (4 shorter events, 0.0 us)
Async XLA Ops:
  7.2 88.0 %copy-start = (bf16[4096,256]{1,0:T(8,128)(2,1)S(1)}, bf16[4096,256]{1,0:T(8,128)(2,1)}, u32[]{:S(2)}) copy-start(bf16[4096,256]{1,0:T(8,128)(2,1)} %param.7) | copy-start | bytes 6291460
  7.2 88.0 %all-gather.3.cloned.1.call-start = ((), (), s32[]{:S(2)}) async-start(), calls=%async_computation.2 | async-start | bytes 2162688 | tf_op jit(solution)/shard_map/all_gather | solution.py:32
  38.8 92.3 %all-gather.5.cloned.1.call-start = ((), (), s32[]{:S(2)}) async-start(), calls=%async_computation.3 | async-start | bytes 1179648 | tf_op jit(solution)/shard_map/all_gather | solution.py:36
  98.2 157.7 %all-reduce.3.cloned.1.call-start = ((), (), s32[]{:S(2)}) async-start(), calls=%async_computation.4 | async-start | bytes 2097152 | tf_op jit(solution)/shard_map/psum | solution.py:48
  131.1 5.0 %copy-start.1 = (bf16[2,1024,256]{2,1,0:T(8,128)(2,1)S(1)}, bf16[2,1024,256]{2,1,0:T(8,128)(2,1)}, u32[]{:S(2)}) copy-start(bf16[2,1024,256]{2,1,0:T(8,128)(2,1)} %all-gather.5.cloned.1.call-done) | copy-start | bytes 3145732
  134.6 1.4 copy-start.2
  137.5 226.9 %reduce-scatter.5.cloned.1.call-start = ((), (), s32[]{:S(2)}) async-start(), calls=%async_computation.6 | async-start | bytes 4325376 | tf_op jit(solution)/shard_map/reduce_scatter | solution.py:70
  138.8 133.1 %copy-start.5 = (f32[1,128,256]{2,1,0:T(8,128)S(1)}, f32[1,128,256]{2,1,0:T(8,128)}, u32[]{:S(2)}) copy-start(f32[1,128,256]{2,1,0:T(8,128)} %get-tuple-element.13) | copy-start | bytes 393220
  275.7 148.1 %reduce-scatter.3.cloned.1.call-start = ((), (), s32[]{:S(2)}) async-start(), calls=%async_computation.5 | async-start | bytes 4718592 | tf_op jit(solution)/shard_map/reduce_scatter | solution.py:77
  280.0 2.7 copy-start.4
  280.0 84.3 %copy-start.3 = (bf16[2,128,128]{2,1,0:T(8,128)(2,1)S(1)}, bf16[2,128,128]{2,1,0:T(8,128)(2,1)}, u32[]{:S(2)}) copy-start(bf16[2,128,128]{2,1,0:T(8,128)(2,1)} %param.4) | copy-start | bytes 196612
  280.0 84.3 %copy-start.6 = (f32[128]{0:T(128)S(1)}, f32[128]{0:T(128)}, u32[]{:S(2)}) copy-start(f32[128]{0:T(128)} %param.5) | copy-start | bytes 1540
  280.0 84.3 %copy-start.7 = (f32[128]{0:T(128)S(1)}, f32[128]{0:T(128)}, u32[]{:S(2)}) copy-start(f32[128]{0:T(128)} %param.6) | copy-start | bytes 1540
Sparse Core Ops, SparseCore 0:
  38.9 56.2 all-gather.2
  98.3 32.7 all-gather.4
  137.6 118.2 all-reduce.2
  275.8 88.5 reduce-scatter.4
  367.3 56.3 reduce-scatter.2
where the time goes:
time: 431 us; the launch traced here: 430 us
  waiting for transfers between devices  249 us (58%)
  blocking collectives  134 us (31%)
  between operations  16.5 us (4%)
  other arithmetic  14.9 us (3%)
  matrix products  13.8 us (3%)
    psum x1, waiting for transfers between devices, shards(): kernel = lax.psum(kernel_part, 'col')  116 us
    psum x1, blocking collectives, shards(): loss = lax.psum(share, ('batch', 'col'))  78.4 us
    all_gather x1, waiting for transfers between devices, shards(): act_full = lax.all_gather(act, 'col', axis=2, tiled=True)  56.4 us
    reduce_scatter x1, waiting for transfers between devices, shards(): lax.psum_scatter(jnp.einsum('vrk,vrj->kj', act_full, dzb, preferred_eleme...  42.5 us
    all_gather x1, waiting for transfers between devices, shards(): z_all = lax.all_gather(z_local, 'batch', axis=1, tiled=True)  32.8 us
    psum x1, blocking collectives, shards(): total = lax.psum(jnp.sum(hidden_float, axis=1), 'batch')  17.3 us
    psum x1, blocking collectives, shards(): lax.psum((jnp.sum(preactivation_gradient, axis=1), jnp.sum(preactivation_...  14.1 us
    psum x1, blocking collectives, shards(): col_total = lax.psum(jnp.sum(summed, axis=1), 'batch')  13.7 us
  transfers between devices with their start and end apart: 5, of which 5 were waited for; matrix products, arithmetic and copies ran while one was open for 3% of the time, Pallas kernels for 0%

commit v1 on v0

--- a/solution.py
+++ b/solution.py
@@ -45,7 +45,7 @@
     zcb_loc = zc_loc.astype(jnp.bfloat16)
     diag = jnp.sum(jnp.square(zcb_all.astype(jnp.float32)), axis=1, keepdims=True)
     kernel_part = jnp.einsum("vrj,vmj->vrm", zcb_loc, zcb_all, preferred_element_type=jnp.float32)
-    kernel = lax.psum(kernel_part, "col")
+    kernel = jnp.sum(jax.lax.all_gather(kernel_part, "col"), 0)
     kernel_b = kernel.astype(jnp.bfloat16)
     denom = float((sample_count - 1) ** 2 * E)
     coef = 4.0 * scale / denom

time: 431 us -> 448 us (1.039)
  other arithmetic: 14.9 us -> 27.7 us
  waiting for transfers between devices: 249 us -> 254 us
    all_gather x0 -> x1, waiting for transfers between devices: none -> 120 us  [shards(): kernel = jnp.sum(jax.lax.all_gather(kernel_part, 'col'), 0)]
    psum x1 -> x0, waiting for transfers between devices: 116 us -> none  [shards(): kernel = lax.psum(kernel_part, 'col')]
    reduce_sum x0 -> x1, other arithmetic: none -> 12.8 us  [shards(): kernel = jnp.sum(jax.lax.all_gather(kernel_part, 'col'), 0)]
  transfers between devices with their start and end apart: 5 -> 5, of which waited for: 5 -> 5; matrix products, arithmetic and copies ran while one was open for 3% -> 2% of each run, Pallas kernels for 0% -> 0%
where the time goes in v1:
time: 448 us; the launch traced here: 447 us
  waiting for transfers between devices  254 us (57%)
  blocking collectives  133 us (30%)
  other arithmetic  27.7 us (6%)
  between operations  16.5 us (4%)
  matrix products  13.8 us (3%)
    all_gather x1, waiting for transfers between devices, shards(): kernel = jnp.sum(jax.lax.all_gather(kernel_part, 'col'), 0)  120 us
    psum x1, blocking collectives, shards(): loss = lax.psum(share, ('batch', 'col'))  77.1 us
    all_gather x1, waiting for transfers between devices, shards(): act_full = lax.all_gather(act, 'col', axis=2, tiled=True)  56.4 us
    reduce_scatter x1, waiting for transfers between devices, shards(): lax.psum_scatter(jnp.einsum('vrk,vrj->kj', act_full, dzb, preferred_eleme...  42.5 us
    all_gather x1, waiting for transfers between devices, shards(): z_all = lax.all_gather(z_local, 'batch', axis=1, tiled=True)  32.8 us
    psum x1, blocking collectives, shards(): total = lax.psum(jnp.sum(hidden_float, axis=1), 'batch')  17.3 us
    psum x1, blocking collectives, shards(): lax.psum((jnp.sum(preactivation_gradient, axis=1), jnp.sum(preactivation_...  14.2 us
    psum x1, blocking collectives, shards(): col_total = lax.psum(jnp.sum(summed, axis=1), 'batch')  13.8 us
  transfers between devices with their start and end apart: 5, of which 5 were waited for; matrix products, arithmetic and copies ran while one was open for 2% of the time, Pallas kernels for 0%

profile of v1, /device:TPU:1, one launch (start us, length us, event | category | flops | bytes accessed | tf_op | source)
XLA Modules:
  0.0 447.2 jit_solution(12151336873196752935)
XLA Ops:
  7.2 0.0 copy-start
  7.2 0.0 all-gather.5.cloned.1.call-start
  7.2 1.0 convert_reduce_fusion.1
  8.2 17.3 %psum.42 = f32[2,128]{1,0:T(2,128)S(1)} all-reduce(f32[2,128]{1,0:T(2,128)S(1)} %convert_reduce_fusion.1), channel_id=1, replica_groups=mesh['batch'=8,'col'=32] {'batch'}, use_global_device_ids=true, to_apply=%region_1.0 | all-reduce | flops 256 | bytes 2048 | tf_op jit(solution)/shard_map/psum | solution.py:23
  25.5 0.9 fusion.32
  26.4 10.8 %psum.43 = f32[2,128]{1,0:T(2,128)S(1)} all-reduce(f32[2,128]{1,0:T(2,128)S(1)} %fusion.32), channel_id=1, replica_groups=mesh['batch'=8,'col'=32] {'batch'}, use_global_device_ids=true, to_apply=%region_3.0 | all-reduce | flops 256 | bytes 2048 | tf_op jit(solution)/shard_map/psum | solution.py:26
  37.2 1.6 fusion.25
  38.8 0.0 all-gather.5.cloned.1.call-update
  38.8 0.0 all-gather.7.cloned.1.call-start
  38.8 56.4 %all-gather.5.cloned.1.call-done = bf16[2,128,4096]{2,1,0:T(8,128)(2,1)} async-done(((bf16[2,128,128]{2,1,0:T(8,128)(2,1)}), bf16[2,128,4096]{2,1,0:T(8,128)(2,1)}) %all-gather.5.cloned.1.call-update) | async-done | bytes 2097168 | tf_op jit(solution)/shard_map/all_gather | solution.py:32
  95.2 0.0 copy-done
  95.2 3.0 fusion.42
  98.2 0.0 all-gather.7.cloned.1.call-update
  98.2 0.0 all-gather.9.cloned.1.call-start
  98.2 32.8 %all-gather.7.cloned.1.call-done = bf16[2,1024,256]{2,1,0:T(8,128)(2,1)} async-done(((bf16[2,128,256]{2,1,0:T(8,128)(2,1)}), bf16[2,1024,256]{2,1,0:T(8,128)(2,1)}) %all-gather.7.cloned.1.call-update) | async-done | bytes 1048592 | tf_op jit(solution)/shard_map/all_gather | solution.py:36
  131.1 0.0 copy-start.1
  131.1 1.5 convert_reduce_fusion
  132.6 2.1 multiply_reduce_fusion
  134.6 0.0 copy-start.3
  134.7 1.4 copy-done.3
  136.0 0.0 copy-done.1
  136.0 1.5 fusion.10
  137.5 0.0 all-gather.9.cloned.1.call-update
  137.5 0.0 reduce-scatter.5.cloned.1.call-start
  137.6 1.3 fusion.41
  138.8 1.3 fusion.37
  140.1 120.2 %all-gather.9.cloned.1.call-done = f32[64,128,1024]{2,1,0:T(8,128)} async-done(((f32[2,128,1024]{2,1,0:T(8,128)}), f32[64,128,1024]{2,1,0:T(8,128)}) %all-gather.9.cloned.1.call-update) | async-done | bytes 33554448 | tf_op jit(solution)/shard_map/all_gather | solution.py:48
  260.3 12.8 %reduce_sum.143 = f32[2,128,1024]{2,1,0:T(8,128)} reduce(f32[32,2,128,1024]{3,2,1,0:T(8,128)} %bitcast.21, f32[]{:T(128)} %constant.24.clone.1), dimensions={0}, to_apply=%region_10.11 | reduce | flops 8126464 | bytes 34603012 | tf_op jit(solution)/shard_map/reduce_sum | solution.py:48
  273.2 0.0 copy-start.5
  273.2 2.4 fusion.43
  275.5 13.8 %psum.45 = f32[2,256]{1,0:T(2,128)S(1)} all-reduce(f32[2,256]{1,0:T(2,128)S(1)} %get-tuple-element.23), channel_id=1, replica_groups=mesh['batch'=8,'col'=32] {'batch'}, use_global_device_ids=true, to_apply=%region_14.15 | all-reduce | flops 512 | bytes 4096 | tf_op jit(solution)/shard_map/psum | solution.py:58
  289.4 0.0 copy-done.5
  289.4 1.0 fusion.13
  290.4 2.7 convolution_bitcast_fusion
  293.1 0.0 reduce-scatter.5.cloned.1.call-update
  293.1 0.0 reduce-scatter.3.cloned.1.call-start
  293.2 4.3 convolution_bitcast_fusion.1
  297.5 0.0 copy-start.2
  297.5 0.0 copy-start.4
  297.5 0.0 copy-start.6
  297.5 0.0 copy-start.7
  297.5 0.0 reduce-scatter.3.cloned.1.call-update
  298.9 0.6 multiply_reduce_fusion.4
  300.1 0.0 copy-done.2
  300.1 0.9 multiply_reduce_fusion.2
  301.7 77.1 %psum.44 = f32[]{:T(128)} all-reduce(f32[]{:T(128)S(6)} %add.81), channel_id=1, replica_groups=mesh['batch'=8,'col'=32] {'batch','col'}, use_global_device_ids=true, to_apply=%region_12.13 | all-reduce | flops 1 | bytes 8 | tf_op jit(solution)/shard_map/psum | solution.py:69
  378.8 2.4 reduce-scatter.5.cloned.1.call-done
  381.2 0.0 copy-done.4
  381.2 0.0 copy-done.6
  381.2 0.0 copy-done.7
  381.2 1.0 fusion.39
  382.2 14.2 %all-reduce = (f32[2,128]{1,0:T(2,128)S(1)}, f32[2,128]{1,0:T(2,128)S(1)}) all-reduce(f32[2,128]{1,0:T(2,128)S(1)} %get-tuple-element.8, f32[2,128]{1,0:T(2,128)S(1)} %get-tuple-element.7), channel_id=1, replica_groups=mesh['batch'=8,'col'=32] {'batch'}, use_global_device_ids=true, to_apply=%region_18.19 | all-reduce | flops 512 | bytes 4096 | tf_op jit(solution)/shard_map/psum | solution.py:84
  396.4 0.5 reduce_sum.147
  396.9 0.5 broadcast_multiply_fusion.3
  397.5 0.7 fusion.31
  398.2 42.5 %reduce-scatter.3.cloned.1.call-done = f32[512,256]{1,0:T(8,128)} async-done(((f32[4096,256]{1,0:T(8,128)}), f32[512,256]{1,0:T(8,128)}) %reduce-scatter.3.cloned.1.call-update) | async-done | bytes 524304 | tf_op jit(solution)/shard_map/reduce_scatter | solution.py:77
  (4 shorter events, 0.0 us)
Async XLA Ops:
  7.2 88.0 %copy-start = (bf16[4096,256]{1,0:T(8,128)(2,1)S(1)}, bf16[4096,256]{1,0:T(8,128)(2,1)}, u32[]{:S(2)}) copy-start(bf16[4096,256]{1,0:T(8,128)(2,1)} %param.7) | copy-start | bytes 6291460
  7.2 88.0 %all-gather.5.cloned.1.call-start = ((), (), s32[]{:S(2)}) async-start(), calls=%async_computation.2 | async-start | bytes 2162688 | tf_op jit(solution)/shard_map/all_gather | solution.py:32
  38.8 92.3 %all-gather.7.cloned.1.call-start = ((), (), s32[]{:S(2)}) async-start(), calls=%async_computation.3 | async-start | bytes 1179648 | tf_op jit(solution)/shard_map/all_gather | solution.py:36
  98.2 162.1 %all-gather.9.cloned.1.call-start = ((), (), s32[]{:S(2)}) async-start(), calls=%async_computation.6 | async-start | bytes 34603008 | tf_op jit(solution)/shard_map/all_gather | solution.py:48
  131.1 5.0 %copy-start.1 = (bf16[2,1024,256]{2,1,0:T(8,128)(2,1)S(1)}, bf16[2,1024,256]{2,1,0:T(8,128)(2,1)}, u32[]{:S(2)}) copy-start(bf16[2,1024,256]{2,1,0:T(8,128)(2,1)} %all-gather.7.cloned.1.call-done) | copy-start | bytes 3145732
  134.6 1.4 copy-start.3
  137.5 243.7 %reduce-scatter.5.cloned.1.call-start = ((), (), s32[]{:S(2)}) async-start(), calls=%async_computation.5 | async-start | bytes 4325376 | tf_op jit(solution)/shard_map/reduce_scatter | solution.py:70
  273.2 16.2 %copy-start.5 = (f32[1,128,256]{2,1,0:T(8,128)S(1)}, f32[1,128,256]{2,1,0:T(8,128)}, u32[]{:S(2)}) copy-start(f32[1,128,256]{2,1,0:T(8,128)} %get-tuple-element.13) | copy-start | bytes 393220
  293.1 147.6 %reduce-scatter.3.cloned.1.call-start = ((), (), s32[]{:S(2)}) async-start(), calls=%async_computation.4 | async-start | bytes 4718592 | tf_op jit(solution)/shard_map/reduce_scatter | solution.py:77
  297.5 2.7 copy-start.2
  297.5 83.7 %copy-start.4 = (bf16[2,128,128]{2,1,0:T(8,128)(2,1)S(1)}, bf16[2,128,128]{2,1,0:T(8,128)(2,1)}, u32[]{:S(2)}) copy-start(bf16[2,128,128]{2,1,0:T(8,128)(2,1)} %param.4) | copy-start | bytes 196612
  297.5 83.7 %copy-start.6 = (f32[128]{0:T(128)S(1)}, f32[128]{0:T(128)}, u32[]{:S(2)}) copy-start(f32[128]{0:T(128)} %param.5) | copy-start | bytes 1540
  297.5 83.7 %copy-start.7 = (f32[128]{0:T(128)S(1)}, f32[128]{0:T(128)}, u32[]{:S(2)}) copy-start(f32[128]{0:T(128)} %param.6) | copy-start | bytes 1540
Sparse Core Ops, SparseCore 0:
  38.9 56.2 all-gather.4
  98.3 32.7 all-gather.6
  137.6 122.6 all-gather.8
  293.2 87.8 reduce-scatter.4
  384.3 56.3 reduce-scatter.2
